TPU v7x, 256 devices: a whole 4x4x8 slice. The times are simulated.
256 devices in a mesh: seq: 64 (over z, x, core), mp: 4 (over y).
Axes of the slice: x: 4, y: 4, z: 8, core: 2. Of those that a mesh axis runs over, the one named last changes fastest.
Arguments:
- x_in: bfloat16 [8192, 8192], P('seq', 'mp'), may hold values from -6 to 6
- gate_z: bfloat16 [8192, 8192], P('seq', 'mp'), may hold values from -6 to 6
- bc_in: bfloat16 [8192, 256], P('seq'), may hold values from -3 to 3
- dt_raw: float32 [8192, 128], P('seq', 'mp'), may hold values from -9 to 0
- a_log: float32 [128], P('mp'), may hold values from -9 to -1
- d_skip: float32 [128], P('mp'), may hold values from 0.5 to 1.5
- conv_x: bfloat16 [4, 8192], P(None, 'mp'), may hold values from -3 to 3
- conv_bc: bfloat16 [4, 256], replicated, may hold values from -3 to 3
- norm_gain: float32 [8192], P('mp'), may hold values from 0.1 to 1.9
- queries: bfloat16 [8192, 4096], P('seq', 'mp'), may hold values from -12 to 12
- key_value_pairs: bfloat16 [2, 8192, 512], P(None, 'seq', 'mp'), may hold values from -12 to 12
Outputs:
- mixer_out: bfloat16 [8192, 8192], P('seq', 'mp')
- attention_out: bfloat16 [8192, 4096], P('seq', 'mp')
All inputs are finite; a program needn't handle non-finite values.
Results may differ from a plain program's by a relative error of at most 0.00085.
Values may be sent and summed in bfloat16 or wider, within the bound.
A program may use at most 192 MiB of HBM per device.

v0:
```python
import jax
import jax.numpy as jnp
from jax import lax
from jax.sharding import PartitionSpec as P

HEAD_P = 64
STATE = 128
CONV = 4
HEAD_WIDTH = 128
D_INNER = 8192


def passed_along(block, axis, distance):
    devices = range(lax.axis_size(axis))
    route = [(i - distance, i) for i in devices if i - distance in devices]
    return lax.ppermute(block, axis, route)


def causal_conv(values, tail, taps):
    joined = jnp.concatenate([tail, values], axis=0).astype(jnp.float32)
    rows = values.shape[0]
    total = jnp.zeros((rows, values.shape[1]), jnp.float32)
    for k in range(CONV):
        total = total + taps[k].astype(jnp.float32)[None, :] * joined[k : k + rows]
    return jax.nn.silu(total)


def local_part(xs, b_map, c_map, step, rate):
    hi = lax.Precision.HIGHEST
    cum = jnp.cumsum(step * rate[None, :], axis=0)
    rows = xs.shape[0]
    order = jnp.arange(rows)
    causal = order[None, :] <= order[:, None]
    inner = jnp.dot(c_map, b_map.T, precision=hi)
    cum_t = cum.T
    diff = cum_t[:, :, None] - cum_t[:, None, :]
    decay = jnp.where(causal[None], jnp.exp(jnp.where(causal[None], diff, 0.0)), 0.0)
    mixing = inner[None] * decay
    scaled = step[:, :, None] * xs
    y_intra = jnp.einsum("hts,shp->thp", mixing, scaled, precision=hi)
    to_end = jnp.exp(cum[-1][None, :] - cum)
    s_loc = jnp.einsum("sn,shp->hnp", b_map, scaled * to_end[:, :, None], precision=hi)
    return (y_intra, s_loc, jnp.exp(cum[-1]), cum)


def attend(rows_q, positions, whole_pairs):
    kv_local = whole_pairs.shape[2] // HEAD_WIDTH
    query_group = rows_q.shape[1] // HEAD_WIDTH // kv_local
    count = rows_q.shape[0]
    heads_q = rows_q.reshape(count, kv_local, query_group, HEAD_WIDTH)
    scale = HEAD_WIDTH ** (-0.5)
    highest = jnp.max(positions)

    def update(carry, block, first):
        running, total, accum = carry
        width = block.shape[1]
        score = (
            jnp.einsum("rkgd,mkd->rkgm", heads_q, block[0], preferred_element_type=jnp.float32)
            * scale
        )
        live = ((first + jnp.arange(width))[None, :] <= positions[:, None])[:, None, None, :]
        peak = jnp.maximum(running, jnp.max(jnp.where(live, score, -1e30), axis=-1))
        weights = jnp.where(live, jnp.exp(score - peak[..., None]), 0.0)
        fade = jnp.exp(running - peak)
        total = total * fade + jnp.sum(weights, axis=-1)
        accum = accum * fade[..., None] + jnp.einsum(
            "rkgm,mkd->rkgd", weights, block[1].astype(jnp.float32), precision=lax.Precision.HIGHEST
        )
        return (peak, total, accum)

    length = whole_pairs.shape[1]
    span = length
    while span > 1024 and span % 2 == 0:
        span = span // 2
    blocks = jnp.moveaxis(whole_pairs.reshape(2, length // span, span, kv_local, HEAD_WIDTH), 1, 0)

    def visit(state, item):
        number, block = item
        first = number * span
        state = lax.cond(first <= highest, lambda c: update(c, block, first), lambda c: c, state)
        return (state, None)

    start_state = (
        jnp.full((count, kv_local, query_group), -1e30, jnp.float32),
        jnp.zeros((count, kv_local, query_group), jnp.float32),
        jnp.zeros((count, kv_local, query_group, HEAD_WIDTH), jnp.float32),
    )
    final_state, _ = lax.scan(
        visit, start_state, (jnp.arange(length // span, dtype=jnp.int32), blocks)
    )
    running, total, accum = final_state
    return (accum / total[..., None]).reshape(count, -1).astype(jnp.bfloat16)


def body(
    x_in, gate_z, bc_in, dt_raw, a_log, d_skip, conv_x, conv_bc, norm_gain, queries, key_value_pairs
):
    rows = x_in.shape[0]
    keep = CONV - 1
    tail_x, tail_bc = passed_along((x_in[rows - keep :], bc_in[rows - keep :]), "seq", 1)
    heads_here = dt_raw.shape[1]
    xs = causal_conv(x_in, tail_x, conv_x).reshape(rows, heads_here, HEAD_P)
    bc_conv = causal_conv(bc_in, tail_bc, conv_bc)
    c_map = bc_conv[:, STATE:]
    step = jax.nn.softplus(dt_raw)
    rate = -jnp.exp(a_log)
    y_intra, s_loc, g_end, cum = local_part(xs, bc_conv[:, :STATE], c_map, step, rate)
    logs = lax.all_gather(cum[-1][None, :], "seq", axis=0, tiled=True)
    mine = lax.axis_index("seq")
    number = logs.shape[0]
    order = jnp.arange(number, dtype=jnp.int32)
    between = jnp.logical_and(order[:, None] < order[None, :], order[None, :] < mine)
    skipped = jnp.dot(between.astype(jnp.float32), logs, precision=lax.Precision.HIGHEST)
    weights = jnp.where((order < mine)[:, None], jnp.exp(jnp.minimum(skipped, 0.0)), 0.0)
    state_in = jnp.einsum(
        "kh,khnp->hnp",
        weights,
        lax.all_gather(s_loc[None], "seq", axis=0, tiled=True),
        precision=lax.Precision.HIGHEST,
    )
    y_inter = jnp.exp(cum)[:, :, None] * jnp.einsum(
        "tn,hnp->thp", c_map, state_in, precision=lax.Precision.HIGHEST
    )
    y_all = y_intra + y_inter + d_skip[None, :, None] * xs
    gated = y_all.reshape(rows, -1) * jax.nn.silu(gate_z.astype(jnp.float32))
    squares = lax.psum(jnp.sum(gated * gated, axis=1), "mp")
    mixer_out = (gated * lax.rsqrt(squares / D_INNER + 1e-05)[:, None] * norm_gain[None, :]).astype(
        jnp.bfloat16
    )
    whole_pairs = lax.all_gather(key_value_pairs, "seq", axis=1, tiled=True)
    place = lax.axis_index("seq")
    positions = place * rows + jnp.arange(rows, dtype=jnp.int32)
    attention_out = attend(queries, positions, whole_pairs)
    return (mixer_out, attention_out)


def solution(mesh):
    placed = (
        P("seq", "mp"),
        P("seq", "mp"),
        P("seq", None),
        P("seq", "mp"),
        P("mp"),
        P("mp"),
        P(None, "mp"),
        P(),
        P("mp"),
        P("seq", "mp"),
        P(None, "seq", "mp"),
    )
    return jax.shard_map(
        body,
        mesh=mesh,
        in_specs=placed,
        out_specs=(P("seq", "mp"), P("seq", "mp")),
        check_vma=False,
    )
```

profile of v0, /device:TPU:233, one launch (start us, length us, event | category | flops | bytes accessed | tf_op | source)
XLA Modules:
  0.0 427.5 jit_solution(13780730352346464074)
XLA Ops:
  25.0 38.1 %all-gather.1 = f32[64,1,32]{2,1,0:T(1,128)S(1)} all-gather(f32[1,1,32]{2,1,0:T(1,128)S(1)} %get-tuple-element.174), channel_id=1, replica_groups=mesh['seq'=64,'mp'=4] {'seq'}, dimensions={0}, use_global_device_ids=true | all-gather | bytes 8320 | tf_op jit(solution)/shard_map/all_gather | solution.py:108
  63.7 25.5 %all-gather.5.cloned.1.call-done = bf16[2,8192,128]{2,1,0:T(8,128)(2,1)} async-done(((bf16[2,128,128]{2,1,0:T(8,128)(2,1)}), bf16[2,8192,128]{2,1,0:T(8,128)(2,1)}) %all-gather.5.cloned.1.call-update) | async-done | bytes 4194320 | tf_op jit(solution)/shard_map/all_gather | solution.py:130
  89.1 4.6 %copy.46 = bf16[8,2,1024,1,128]{4,2,3,1,0:T(8,128)(2,1)} copy(bf16[8,2,1024,1,128]{4,2,0,1,3:T(8,128)(2,1)} %bitcast.110) | data formatting | bytes 8388608
  93.8 93.6 %while.15 = (s32[]{:T(128)}, f32[128,1,8]{0,2,1:T(8,128)S(1)}, f32[128,1,8]{0,2,1:T(8,128)S(1)}, f32[128,1,8,128]{0,3,2,1:T(8,128)S(1)}, s32[8]{0:T(128)S(1)}, /...) while((s32[]{:T(128)}, f32[128,1,8]{0,2,1:T(8,128)S(1)}, ...), condition=%wide.region_9.10_spmd.clone, body=%wide.region_4.9_spmd.clone.sunk | while | flops 1889931392 | bytes 31796552 | solution.py:88
  95.6 9.8 %conditional.3 = ((f32[128,1,8]{0,2,1:T(8,128)S(1)}, f32[128,1,8]{0,2,1:T(8,128)S(1)}, f32[128,1,8,128]{0,3,2,1:T(8,128)S(1)})) conditional(s32[]{:T(128)} %convert_element_type.67, (f32[128,1,8]{0,2,1:T(8,128)S(1)}, f32[128,1,8]{0,2,1:T(8,128)S(1)}, f32[128,1,8,128]{0,3,2,1:T(8,128)S(1)}) %tuple.52, (s32[]{:T(128)}, s32[]{:T(128)}, ...), branch_computations={%region_5.5_spmd, %region_6.8_spmd} | conditional | flops 1889931392 | bytes 31795796 | solution.py:80
  100.4 5.0 %fusion.16 = f32[128,1,8,128]{0,3,2,1:T(8,128)S(1)} fusion(f32[1024,128,8]{1,0,2:T(8,128)} %copy-done, f32[128,8]{0,1:T(8,128)S(1)} %bitcast.114, pred[128,1024]{0,1:T(8,128)(4,1)S(1)} %broadcast_compare_fusion, f32[128,1,8,128]{0,3,2,1:T(8,128)S(1)} %get-tuple-element.84, bf16[8,2,1024,1,128]{4,2,3,1,0:T(8,128)(2,1)} %get-tuple-element.80, ...), kind=kOutput, calls=%fused_computation.14 | convolution fusion | flops 1614020608 | bytes 5644804 | tf_op jit(solution)/shard_map/while/body/eval_jaxpr/cond/branch_1_fun/rkgm,mkd->rkgd/dot_general | solution.py:66
  107.2 9.7 %conditional.3 = ((f32[128,1,8]{0,2,1:T(8,128)S(1)}, f32[128,1,8]{0,2,1:T(8,128)S(1)}, f32[128,1,8,128]{0,3,2,1:T(8,128)S(1)})) conditional(s32[]{:T(128)} %convert_element_type.67, (f32[128,1,8]{0,2,1:T(8,128)S(1)}, f32[128,1,8]{0,2,1:T(8,128)S(1)}, f32[128,1,8,128]{0,3,2,1:T(8,128)S(1)}) %tuple.52, (s32[]{:T(128)}, s32[]{:T(128)}, ...), branch_computations={%region_5.5_spmd, %region_6.8_spmd} | conditional | flops 1889931392 | bytes 31795796 | solution.py:80
  112.0 4.9 %fusion.16 = f32[128,1,8,128]{0,3,2,1:T(8,128)S(1)} fusion(f32[1024,128,8]{1,0,2:T(8,128)} %copy-done, f32[128,8]{0,1:T(8,128)S(1)} %bitcast.114, pred[128,1024]{0,1:T(8,128)(4,1)S(1)} %broadcast_compare_fusion, f32[128,1,8,128]{0,3,2,1:T(8,128)S(1)} %get-tuple-element.84, bf16[8,2,1024,1,128]{4,2,3,1,0:T(8,128)(2,1)} %get-tuple-element.80, ...), kind=kOutput, calls=%fused_computation.14 | convolution fusion | flops 1614020608 | bytes 5644804 | tf_op jit(solution)/shard_map/while/body/eval_jaxpr/cond/branch_1_fun/rkgm,mkd->rkgd/dot_general | solution.py:66
  118.8 9.7 %conditional.3 = ((f32[128,1,8]{0,2,1:T(8,128)S(1)}, f32[128,1,8]{0,2,1:T(8,128)S(1)}, f32[128,1,8,128]{0,3,2,1:T(8,128)S(1)})) conditional(s32[]{:T(128)} %convert_element_type.67, (f32[128,1,8]{0,2,1:T(8,128)S(1)}, f32[128,1,8]{0,2,1:T(8,128)S(1)}, f32[128,1,8,128]{0,3,2,1:T(8,128)S(1)}) %tuple.52, (s32[]{:T(128)}, s32[]{:T(128)}, ...), branch_computations={%region_5.5_spmd, %region_6.8_spmd} | conditional | flops 1889931392 | bytes 31795796 | solution.py:80
  123.6 4.8 %fusion.16 = f32[128,1,8,128]{0,3,2,1:T(8,128)S(1)} fusion(f32[1024,128,8]{1,0,2:T(8,128)} %copy-done, f32[128,8]{0,1:T(8,128)S(1)} %bitcast.114, pred[128,1024]{0,1:T(8,128)(4,1)S(1)} %broadcast_compare_fusion, f32[128,1,8,128]{0,3,2,1:T(8,128)S(1)} %get-tuple-element.84, bf16[8,2,1024,1,128]{4,2,3,1,0:T(8,128)(2,1)} %get-tuple-element.80, ...), kind=kOutput, calls=%fused_computation.14 | convolution fusion | flops 1614020608 | bytes 5644804 | tf_op jit(solution)/shard_map/while/body/eval_jaxpr/cond/branch_1_fun/rkgm,mkd->rkgd/dot_general | solution.py:66
  130.3 9.7 %conditional.3 = ((f32[128,1,8]{0,2,1:T(8,128)S(1)}, f32[128,1,8]{0,2,1:T(8,128)S(1)}, f32[128,1,8,128]{0,3,2,1:T(8,128)S(1)})) conditional(s32[]{:T(128)} %convert_element_type.67, (f32[128,1,8]{0,2,1:T(8,128)S(1)}, f32[128,1,8]{0,2,1:T(8,128)S(1)}, f32[128,1,8,128]{0,3,2,1:T(8,128)S(1)}) %tuple.52, (s32[]{:T(128)}, s32[]{:T(128)}, ...), branch_computations={%region_5.5_spmd, %region_6.8_spmd} | conditional | flops 1889931392 | bytes 31795796 | solution.py:80
  135.1 4.8 %fusion.16 = f32[128,1,8,128]{0,3,2,1:T(8,128)S(1)} fusion(f32[1024,128,8]{1,0,2:T(8,128)} %copy-done, f32[128,8]{0,1:T(8,128)S(1)} %bitcast.114, pred[128,1024]{0,1:T(8,128)(4,1)S(1)} %broadcast_compare_fusion, f32[128,1,8,128]{0,3,2,1:T(8,128)S(1)} %get-tuple-element.84, bf16[8,2,1024,1,128]{4,2,3,1,0:T(8,128)(2,1)} %get-tuple-element.80, ...), kind=kOutput, calls=%fused_computation.14 | convolution fusion | flops 1614020608 | bytes 5644804 | tf_op jit(solution)/shard_map/while/body/eval_jaxpr/cond/branch_1_fun/rkgm,mkd->rkgd/dot_general | solution.py:66
  141.8 9.6 %conditional.3 = ((f32[128,1,8]{0,2,1:T(8,128)S(1)}, f32[128,1,8]{0,2,1:T(8,128)S(1)}, f32[128,1,8,128]{0,3,2,1:T(8,128)S(1)})) conditional(s32[]{:T(128)} %convert_element_type.67, (f32[128,1,8]{0,2,1:T(8,128)S(1)}, f32[128,1,8]{0,2,1:T(8,128)S(1)}, f32[128,1,8,128]{0,3,2,1:T(8,128)S(1)}) %tuple.52, (s32[]{:T(128)}, s32[]{:T(128)}, ...), branch_computations={%region_5.5_spmd, %region_6.8_spmd} | conditional | flops 1889931392 | bytes 31795796 | solution.py:80
  146.6 4.8 %fusion.16 = f32[128,1,8,128]{0,3,2,1:T(8,128)S(1)} fusion(f32[1024,128,8]{1,0,2:T(8,128)} %copy-done, f32[128,8]{0,1:T(8,128)S(1)} %bitcast.114, pred[128,1024]{0,1:T(8,128)(4,1)S(1)} %broadcast_compare_fusion, f32[128,1,8,128]{0,3,2,1:T(8,128)S(1)} %get-tuple-element.84, bf16[8,2,1024,1,128]{4,2,3,1,0:T(8,128)(2,1)} %get-tuple-element.80, ...), kind=kOutput, calls=%fused_computation.14 | convolution fusion | flops 1614020608 | bytes 5644804 | tf_op jit(solution)/shard_map/while/body/eval_jaxpr/cond/branch_1_fun/rkgm,mkd->rkgd/dot_general | solution.py:66
  153.2 10.9 %conditional.3 = ((f32[128,1,8]{0,2,1:T(8,128)S(1)}, f32[128,1,8]{0,2,1:T(8,128)S(1)}, f32[128,1,8,128]{0,3,2,1:T(8,128)S(1)})) conditional(s32[]{:T(128)} %convert_element_type.67, (f32[128,1,8]{0,2,1:T(8,128)S(1)}, f32[128,1,8]{0,2,1:T(8,128)S(1)}, f32[128,1,8,128]{0,3,2,1:T(8,128)S(1)}) %tuple.52, (s32[]{:T(128)}, s32[]{:T(128)}, ...), branch_computations={%region_5.5_spmd, %region_6.8_spmd} | conditional | flops 1889931392 | bytes 31795796 | solution.py:80
  158.1 6.1 %fusion.16 = f32[128,1,8,128]{0,3,2,1:T(8,128)S(1)} fusion(f32[1024,128,8]{1,0,2:T(8,128)} %copy-done, f32[128,8]{0,1:T(8,128)S(1)} %bitcast.114, pred[128,1024]{0,1:T(8,128)(4,1)S(1)} %broadcast_compare_fusion, f32[128,1,8,128]{0,3,2,1:T(8,128)S(1)} %get-tuple-element.84, bf16[8,2,1024,1,128]{4,2,3,1,0:T(8,128)(2,1)} %get-tuple-element.80, ...), kind=kOutput, calls=%fused_computation.14 | convolution fusion | flops 1614020608 | bytes 5644804 | tf_op jit(solution)/shard_map/while/body/eval_jaxpr/cond/branch_1_fun/rkgm,mkd->rkgd/dot_general | solution.py:66
  166.0 9.6 %conditional.3 = ((f32[128,1,8]{0,2,1:T(8,128)S(1)}, f32[128,1,8]{0,2,1:T(8,128)S(1)}, f32[128,1,8,128]{0,3,2,1:T(8,128)S(1)})) conditional(s32[]{:T(128)} %convert_element_type.67, (f32[128,1,8]{0,2,1:T(8,128)S(1)}, f32[128,1,8]{0,2,1:T(8,128)S(1)}, f32[128,1,8,128]{0,3,2,1:T(8,128)S(1)}) %tuple.52, (s32[]{:T(128)}, s32[]{:T(128)}, ...), branch_computations={%region_5.5_spmd, %region_6.8_spmd} | conditional | flops 1889931392 | bytes 31795796 | solution.py:80
  170.8 4.8 %fusion.16 = f32[128,1,8,128]{0,3,2,1:T(8,128)S(1)} fusion(f32[1024,128,8]{1,0,2:T(8,128)} %copy-done, f32[128,8]{0,1:T(8,128)S(1)} %bitcast.114, pred[128,1024]{0,1:T(8,128)(4,1)S(1)} %broadcast_compare_fusion, f32[128,1,8,128]{0,3,2,1:T(8,128)S(1)} %get-tuple-element.84, bf16[8,2,1024,1,128]{4,2,3,1,0:T(8,128)(2,1)} %get-tuple-element.80, ...), kind=kOutput, calls=%fused_computation.14 | convolution fusion | flops 1614020608 | bytes 5644804 | tf_op jit(solution)/shard_map/while/body/eval_jaxpr/cond/branch_1_fun/rkgm,mkd->rkgd/dot_general | solution.py:66
  177.5 9.8 %conditional.3 = ((f32[128,1,8]{0,2,1:T(8,128)S(1)}, f32[128,1,8]{0,2,1:T(8,128)S(1)}, f32[128,1,8,128]{0,3,2,1:T(8,128)S(1)})) conditional(s32[]{:T(128)} %convert_element_type.67, (f32[128,1,8]{0,2,1:T(8,128)S(1)}, f32[128,1,8]{0,2,1:T(8,128)S(1)}, f32[128,1,8,128]{0,3,2,1:T(8,128)S(1)}) %tuple.52, (s32[]{:T(128)}, s32[]{:T(128)}, ...), branch_computations={%region_5.5_spmd, %region_6.8_spmd} | conditional | flops 1889931392 | bytes 31795796 | solution.py:80
  182.3 5.0 %fusion.16 = f32[128,1,8,128]{0,3,2,1:T(8,128)S(1)} fusion(f32[1024,128,8]{1,0,2:T(8,128)} %copy-done, f32[128,8]{0,1:T(8,128)S(1)} %bitcast.114, pred[128,1024]{0,1:T(8,128)(4,1)S(1)} %broadcast_compare_fusion, f32[128,1,8,128]{0,3,2,1:T(8,128)S(1)} %get-tuple-element.84, bf16[8,2,1024,1,128]{4,2,3,1,0:T(8,128)(2,1)} %get-tuple-element.80, ...), kind=kOutput, calls=%fused_computation.14 | convolution fusion | flops 1614020608 | bytes 5644804 | tf_op jit(solution)/shard_map/while/body/eval_jaxpr/cond/branch_1_fun/rkgm,mkd->rkgd/dot_general | solution.py:66
  188.3 136.3 %all-gather.7.cloned.1.call-done = f32[2048,128,64]{1,2,0:T(8,128)} async-done(((f32[32,128,64]{1,2,0:T(8,128)}), f32[2048,128,64]{1,2,0:T(8,128)}) %all-gather.7.cloned.1.call-update) | async-done | bytes 67108880 | tf_op jit(solution)/shard_map/all_gather | solution.py:118
  324.5 82.2 %fusion.26 = f32[32,1,128,64]{2,1,3,0:T(1,128)S(1)} fusion(f32[64,32,1,1]{0,2,3,1:T(1,128)S(1)} %bitcast.122, f32[64,32,128,64]{2,3,1,0:T(8,128)} %bitcast.33), kind=kOutput, calls=%fused_computation.30 | convolution fusion | flops 201326592 | bytes 68165632 | tf_op jit(solution)/shard_map/kh,khnp->hnp/dot_general | solution.py:115
  407.8 4.3 %fusion.40 = f32[128,32,64]{0,2,1:T(8,128)S(1)} fusion(f32[128,32,64]{0,2,1:T(8,128)S(1)} %bitcast.112, f32[128,32,64]{0,2,1:T(8,128)S(1)} %bitcast.116, f32[32,128]{1,0:T(8,128)S(1)} %copy.40, f32[128,128]{1,0:T(8,128)S(1)} %fusion.68, pred[128,128]{1,0:T(8,128)(4,1)S(1)} %iota_compare_fusion, f32[32]{0:T(128)S(1)} %copy-done.4, f32[128,32]{0,1:T(8,128)S(1)} %copy.42, ...), kind=kOutput, calls=%fused_computation.43 | convolution fusion | flops 406061056 | bytes 3276928 | tf_op jit(solution)/shard_map/hts,shp->thp/dot_general | solution.py:40
  412.8 6.6 %psum.7 = f32[128]{0:T(128)S(1)} all-reduce(f32[128]{0:T(128)S(1)} %multiply_reduce_fusion), channel_id=1, replica_groups=mesh['seq'=64,'mp'=4] {'mp'}, use_global_device_ids=true, to_apply=%region_2.3 | all-reduce | flops 128 | bytes 1024 | tf_op jit(solution)/shard_map/psum | solution.py:126
  (149 shorter events, 64.6 us)
Async XLA Ops:
  7.2 82.0 %all-gather.5.cloned.1.call-start = ((), (), s32[]{:S(2)}) async-start(), calls=%async_computation | async-start | bytes 4259840 | tf_op jit(solution)/shard_map/all_gather | solution.py:130
  7.9 316.6 %all-gather.7.cloned.1.call-start = ((), (), s32[]{:S(2)}) async-start(), calls=%async_computation.1 | async-start | bytes 68157440 | tf_op jit(solution)/shard_map/all_gather | solution.py:118
  8.6 9.9 %collective-permute-start.1 = (bf16[3,256]{1,0:T(4,128)(2,1)S(1)}, bf16[3,256]{1,0:T(4,128)(2,1)S(1)}, u32[]{:S(2)}, u32[]{:S(2)}) collective-permute-start(bf16[3,256]{1,0:T(4,128)(2,1)S(1)} %slice.86), channel_id=1, source_target_pairs={{0,4},{4,8},{8,12},{12,16},{16,20},{20,24},{24,28},{28,32},{32,36}... | collective-permute-start | bytes 4616 | tf_op jit(solution)/shard_map/ppermute | solution.py:16
  13.1 6.5 %collective-permute-start = (bf16[3,2048]{1,0:T(4,128)(2,1)S(1)}, bf16[3,2048]{1,0:T(4,128)(2,1)S(1)}, u32[]{:S(2)}, u32[]{:S(2)}) collective-permute-start(bf16[3,2048]{1,0:T(4,128)(2,1)S(1)} %slice.77), channel_id=1, source_target_pairs={{0,4},{4,8},{8,12},{12,16},{16,20},{20,24},{24,28},{28,32},{32,36}... | collective-permute-start | bytes 36872 | tf_op jit(solution)/shard_map/ppermute | solution.py:16
  20.8 3.9 copy-start.2
  97.6 2.0 copy-start
  109.2 2.0 copy-start
  120.8 2.0 copy-start
  132.3 2.0 copy-start
  143.8 2.0 copy-start
  155.2 2.0 copy-start
  168.0 2.0 copy-start
  179.5 2.0 copy-start
  324.5 83.2 %copy-start.4 = (f32[32]{0:T(128)S(1)}, f32[32]{0:T(128)}, u32[]{:S(2)}) copy-start(f32[32]{0:T(128)} %param.20) | copy-start | bytes 388
  406.7 5.7 %copy-start.1 = (bf16[128,2048]{1,0:T(8,128)(2,1)S(1)}, bf16[128,2048]{1,0:T(8,128)(2,1)}, u32[]{:S(2)}) copy-start(bf16[128,2048]{1,0:T(8,128)(2,1)} %param.16) | copy-start | bytes 1572868
  407.7 11.7 %copy-start.3 = (f32[2048]{0:T(1024)S(1)}, f32[2048]{0:T(1024)}, u32[]{:S(2)}) copy-start(f32[2048]{0:T(1024)} %param.23) | copy-start | bytes 24580
Sparse Core Ops, SparseCore 0:
  10.8 78.3 all-gather.4
  91.9 232.5 all-gather.6
where the time goes:
time: 436 us; the launch traced here: 427 us
  waiting for transfers between devices  162 us (37%)
  matrix products  144 us (33%)
  blocking collectives  44.7 us (10%)
  local copies, waits for them, and re-layouts  28.3 us (6%)
  other arithmetic  17.3 us (4%)
  between operations  14.3 us (3%)
  loops' own time  10.9 us (2%)
  starting transfers between devices  5.66 us (1%)
    all_gather x1, waiting for transfers between devices, body(): lax.all_gather(s_loc[None], 'seq', axis=0, tiled=True)  136 us
    dot_general x1, matrix products, body(): jnp.einsum('kh,khnp->hnp', weights, lax.all_gather(s_loc[None], 'seq', ax...  82.2 us
    dot_general x8, matrix products, update(): jnp.einsum('rkgm,mkd->rkgd', weights, block[1].astype(jnp.float32), preci...  40.2 us
    all_gather x1, blocking collectives, body(): logs = lax.all_gather(cum[-1][None, :], 'seq', axis=0, tiled=True)  38.1 us
    all_gather x1, waiting for transfers between devices, body(): whole_pairs = lax.all_gather(key_value_pairs, 'seq', axis=1, tiled=True)  25.5 us
    cond x24, local copies, waits for them, and re-layouts  15.5 us
    dot_general x8, matrix products, update(): jnp.einsum('rkgd,mkd->rkgm', heads_q, block[0], preferred_element_type=jn...  13.7 us
    another operation x1, loops' own time, attend(): lax.scan(visit, start_state, (jnp.arange(length // span, dtype=jnp.int32)...  10.3 us
  transfers between devices with their start and end apart: 4, of which 2 were waited for; matrix products, arithmetic and copies ran while one was open for 20% of the time, Pallas kernels for 0%

commit v1 on v0

v1 whole, which is shorter than its diff:
```python
import jax
import jax.numpy as jnp
from jax import lax
from jax.experimental import pallas as pl
from jax.experimental.pallas import tpu as pltpu
from jax.sharding import PartitionSpec as P

HEAD_P = 64
STATE = 128
CONV = 4
HEAD_WIDTH = 128
D_INNER = 8192

ROWS = 128
PLANE = 8
PLANES = 8
CHIPS = 4
TOK = PLANE * ROWS
WIDE = 256
OWN_HEADS = 4
TAIL = 16
Q_HEADS = 8
SPLIT = 16

MESH = pl.DeviceIdType.MESH
F32 = jnp.float32
BF16 = jnp.bfloat16
HI = lax.Precision.HIGHEST
NN = (((1,), (0,)), ((), ()))
NT = (((1,), (1,)), ((), ()))


def dot1(a, b, dims=NN):
    return lax.dot_general(a, b, dims, preferred_element_type=F32)


def exact(a, b, dims=NN):
    return lax.dot_general(a, b, dims, precision=HI, preferred_element_type=F32)


def halves(v):
    high = v.astype(BF16)
    return high, (v - high.astype(F32)).astype(BF16)


def dot3(a, b, dims=NN):
    ah, al = halves(a)
    bh, bl = halves(b)
    return dot1(ah, bh, dims) + (dot1(ah, bl, dims) + dot1(al, bh, dims))


def silu(v):
    return v / (1.0 + jnp.exp(-v))


def softplus(v):
    u = jnp.exp(-jnp.abs(v))
    w = 1.0 + u
    small = w == 1.0
    tail = jnp.where(small, u, jnp.log(w) * (u / jnp.where(small, 1.0, w - 1.0)))
    return jnp.maximum(v, 0.0) + tail


def kernel(
    x_hbm,
    gate_hbm,
    bc_hbm,
    dt_ref,
    alog_ref,
    dskip_ref,
    taps_x_ref,
    taps_bc_ref,
    gain_ref,
    q_hbm,
    kv_hbm,
    mix_hbm,
    att_hbm,
    kvbuf,
    xbuf,
    gbuf,
    bcbuf,
    dtsrc,
    dtbuf,
    xs_ref,
    b_ref,
    c_ref,
    cum_ref,
    step_ref,
    lead_ref,
    states,
    y_ref,
    tsrc,
    trecv,
    psrc,
    precv,
    ss_ref,
    ssm_ref,
    ss2_ref,
    ssp_ref,
    osrc,
    qbuf,
    peak_ref,
    acc_ref,
    obuf,
    local_sem,
    q_sem,
    x_s,
    x_r,
    dt_s,
    dt_r,
    g_s,
    g_r,
    bcx_s,
    bcx_r,
    bcp_s,
    bcp_r,
    kvx_s,
    kvx_r,
    kvp_s,
    kvp_r,
    up_s,
    up_r,
    dn_s,
    dn_r,
    tx_s,
    tb_s,
    tail_r,
    t_s,
    t_r,
    p_s,
    p_r,
    m_s,
    m_r,
    n_s,
    n_r,
    o_s,
    o_r,
):
    me = lax.axis_index("seq")
    mine_mp = lax.axis_index("mp")
    z = me // PLANE
    j = me % PLANE
    xc = j // 2
    core = j % 2
    base = z * PLANE
    partner = base + xc * 2 + (1 - core)
    above = ((z + 1) % PLANES) * PLANE
    below = ((z + PLANES - 1) % PLANES) * PLANE

    def remote(src, dst, ss, rs, seq):
        return pltpu.make_async_remote_copy(
            src_ref=src, dst_ref=dst, send_sem=ss, recv_sem=rs, device_id={"seq": seq}, device_id_type=MESH
        )

    def in_plane(r):
        return base + (j + r) % PLANE

    def on_chip(r):
        return base + ((xc + r) % CHIPS) * 2 + core

    def in_column(r):
        return ((z + r) % PLANES) * PLANE + j

    def from_plane(r):
        return (j + PLANE - r) % PLANE

    def from_column(r):
        return (z + PLANES - r) % PLANES

    barrier = pltpu.get_barrier_semaphore()

    def greet(seq):
        pl.semaphore_signal(barrier, inc=1, device_id={"seq": seq}, device_id_type=MESH)

    @pl.loop(1, PLANE)
    def _(r):
        greet(in_plane(r))
        greet(in_column(r))

    @pl.loop(1, 4)
    def _(r):
        pl.semaphore_signal(barrier, inc=1, device_id={"mp": (mine_mp + r) % 4}, device_id_type=MESH)

    @pl.when(j == PLANE - 1)
    def _():
        @pl.loop(0, PLANE - 1)
        def _(d):
            greet(above + d)

    @pl.when(j != PLANE - 1)
    def _():
        greet(below + PLANE - 1)

    dt_t = jnp.transpose(dt_ref[...])
    for d in range(PLANE):
        dtsrc[d, pl.ds(0, OWN_HEADS), :] = dt_t[d * OWN_HEADS : (d + 1) * OWN_HEADS]
        dtsrc[d, pl.ds(OWN_HEADS, OWN_HEADS), :] = jnp.zeros((OWN_HEADS, ROWS), F32)

    my_rows = pl.ds(pl.multiple_of(TAIL + j * ROWS, TAIL), ROWS)
    kv_off = pl.multiple_of(core * 512 + xc * ROWS, ROWS)
    kv_mine = kvbuf.at[z, :, pl.ds(kv_off, ROWS), :]

    def cols(d):
        return pl.ds(pl.multiple_of(d * WIDE, WIDE), WIDE)

    local = [
        pltpu.make_async_copy(kv_hbm, kv_mine, local_sem.at[0]),
        pltpu.make_async_copy(bc_hbm, bcbuf.at[my_rows, :], local_sem.at[1]),
        pltpu.make_async_copy(x_hbm.at[:, cols(j)], xbuf.at[my_rows, :], local_sem.at[2]),
        pltpu.make_async_copy(dtsrc.at[j], dtbuf.at[j], local_sem.at[3]),
        pltpu.make_async_copy(
            gate_hbm.at[:, cols(j)], gbuf.at[pl.ds(pl.multiple_of(j * ROWS, ROWS), ROWS), :], local_sem.at[4]
        ),
    ]
    for copy in local:
        copy.start()
    for h in range(Q_HEADS):
        pltpu.make_async_copy(q_hbm.at[:, pl.ds(h * 128, 128)], qbuf.at[pl.ds(h * ROWS, ROWS), :], q_sem.at[h]).start()

    pl.semaphore_wait(barrier, 2 * (PLANE - 1) + 3 + jnp.where(j == PLANE - 1, PLANE - 1, 1))

    def kvx(r):
        return remote(kv_hbm, kv_mine, kvx_s.at[r], kvx_r.at[r], on_chip(r))

    def kvx_in(r):
        off = pl.multiple_of(core * 512 + ((xc + CHIPS - r) % CHIPS) * ROWS, ROWS)
        slot = kvbuf.at[z, :, pl.ds(off, ROWS), :]
        return remote(slot, slot, kvx_s.at[r], kvx_r.at[r], partner)

    def bcx(r):
        return remote(bc_hbm, bcbuf.at[my_rows, :], bcx_s.at[r], bcx_r.at[r], on_chip(r))

    def bc_slot(r, half):
        owner = ((xc + CHIPS - r) % CHIPS) * 2 + half
        return bcbuf.at[pl.ds(pl.multiple_of(TAIL + owner * ROWS, TAIL), ROWS), :]

    def bcx_in(r):
        slot = bc_slot(r, core)
        return remote(slot, slot, bcx_s.at[r], bcx_r.at[r], partner)

    def bcp(r):
        slot = bc_slot(r, core)
        return remote(slot, slot, bcp_s.at[r], bcp_r.at[r], partner)

    def bcp_in(r):
        slot = bc_slot(r, 1 - core)
        return remote(slot, slot, bcp_s.at[r], bcp_r.at[r], partner)

    bcp_own = remote(bc_hbm, bcbuf.at[my_rows, :], bcp_s.at[0], bcp_r.at[0], partner)

    def xa(r):
        return remote(
            x_hbm.at[:, cols((j + r) % PLANE)], xbuf.at[my_rows, :], x_s.at[r], x_r.at[r], in_plane(r)
        )

    def xa_in(r):
        slot = xbuf.at[pl.ds(pl.multiple_of(TAIL + from_plane(r) * ROWS, TAIL), ROWS), :]
        return remote(slot, slot, x_s.at[r], x_r.at[r], in_plane(r))

    def dta(r):
        return remote(dtsrc.at[(j + r) % PLANE], dtbuf.at[j], dt_s.at[r], dt_r.at[r], in_plane(r))

    def dta_in(r):
        slot = dtbuf.at[from_plane(r)]
        return remote(slot, slot, dt_s.at[r], dt_r.at[r], in_plane(r))

    def ga(r):
        slot = gbuf.at[pl.ds(pl.multiple_of(j * ROWS, ROWS), ROWS), :]
        return remote(gate_hbm.at[:, cols((j + r) % PLANE)], slot, g_s.at[r], g_r.at[r], in_plane(r))

    def ga_in(r):
        slot = gbuf.at[pl.ds(pl.multiple_of(from_plane(r) * ROWS, ROWS), ROWS), :]
        return remote(slot, slot, g_s.at[r], g_r.at[r], in_plane(r))

    last_rows = pl.ds(ROWS - TAIL, TAIL)

    def tail_x(d):
        return remote(
            x_hbm.at[last_rows, cols(d)], xbuf.at[pl.ds(0, TAIL), :], tx_s.at[d], tail_r.at[0], above + d
        )

    def tail_bc(d):
        return remote(
            bc_hbm.at[last_rows, :], bcbuf.at[pl.ds(0, TAIL), :], tb_s.at[d], tail_r.at[1], above + d
        )

    @pl.loop(1, CHIPS)
    def _(r):
        kvx(r).start()

    @pl.loop(1, CHIPS)
    def _(r):
        bcx(r).start()

    bcp_own.start()

    @pl.when(j == PLANE - 1)
    def _():
        @pl.loop(0, PLANE)
        def _(d):
            tail_x(d).start()
            tail_bc(d).start()

    @pl.loop(1, PLANE)
    def _(r):
        dta(r).start()
        xa(r).start()

    @pl.loop(1, PLANE)
    def _(r):
        ga(r).start()

    def column(zz, half):
        return kvbuf.at[zz, :, pl.ds(pl.multiple_of(half * 512, 512), 512), :]

    def up(s):
        part = column((z + PLANES - s + 1) % PLANES, core)
        return remote(part, part, up_s.at[s], up_r.at[s], above + j)

    def up_in(s):
        part = column((z + PLANES - s) % PLANES, core)
        return remote(part, part, up_s.at[s], up_r.at[s], above + j)

    def down(s):
        part = column((z + s - 1) % PLANES, core)
        return remote(part, part, dn_s.at[s], dn_r.at[s], below + j)

    def down_in(s):
        part = column((z + s) % PLANES, core)
        return remote(part, part, dn_s.at[s], dn_r.at[s], below + j)

    def share(zz, i):
        part = column(zz, core)
        return remote(part, part, kvp_s.at[i], kvp_r.at[i], partner)

    def share_in(zz, i):
        part = column(zz, 1 - core)
        return remote(part, part, kvp_s.at[i], kvp_r.at[i], partner)

    local[0].wait()

    @pl.loop(1, CHIPS)
    def _(r):
        kvx_in(r).wait_recv()

    up(1).start()
    down(1).start()
    share(z, 0).start()

    def ring_step(s):
        up_in(s).wait_recv()
        if s < 4:
            up(s + 1).start()
        share((z + PLANES - s) % PLANES, s).start()
        if s < 4:
            down_in(s).wait_recv()
            if s < 3:
                down(s + 1).start()
            share((z + s) % PLANES, 8 - s).start()

    factor = (HEAD_WIDTH ** (-0.5)) * 1.4426950408889634
    tile = 256

    def attend(zz, own):
        @pl.loop(0, Q_HEADS * ROWS // tile)
        def _(t):
            rows = pl.ds(pl.multiple_of(t * tile, tile), tile)
            q = qbuf[rows, :]
            score = dot1(q, kvbuf[zz, 0], NT)
            if own:
                lane = lax.broadcasted_iota(jnp.int32, (1, TOK), 1)
                spot = (((lane % 512) // ROWS) * 2 + lane // 512) * ROWS + lane % ROWS
                place = j * ROWS + lax.broadcasted_iota(jnp.int32, (tile, 1), 0) % ROWS
                score = jnp.where(spot <= place, score, -1e30)
                peak = jnp.max(score, axis=1, keepdims=True)
            else:
                before = peak_ref[rows, :][:, :1]
                peak = jnp.maximum(before, jnp.max(score, axis=1, keepdims=True))
            weights = jnp.exp2((score - peak) * factor)
            high, low = halves(weights)
            value = jnp.concatenate([kvbuf[zz, 1], jnp.ones((TOK, HEAD_WIDTH), BF16)], axis=1)
            part = dot1(high, value) + dot1(low, value)
            if own:
                acc_ref[rows, :] = part
            else:
                acc_ref[rows, :] = acc_ref[rows, :] * jnp.exp2((before - peak) * factor) + part
            peak_ref[rows, :] = jnp.broadcast_to(peak, (tile, HEAD_WIDTH))

    def attend_step(i):
        zz = (z + PLANES - i) % PLANES
        share_in(zz, i).wait_recv()

        @pl.when(i <= z)
        def _():
            attend(zz, False)

    for h in range(Q_HEADS):
        pltpu.make_async_copy(q_hbm.at[:, pl.ds(h * 128, 128)], qbuf.at[pl.ds(h * ROWS, ROWS), :], q_sem.at[h]).wait()
    share_in(z, 0).wait_recv()

    local[1].wait()

    @pl.loop(1, CHIPS)
    def _(r):
        bcx_in(r).wait_recv()
        bcp(r).start()

    attend(z, True)

    @pl.loop(0, CHIPS)
    def _(r):
        bcp_in(r).wait_recv()

    tail_x_in = remote(
        xbuf.at[pl.ds(0, TAIL), :], xbuf.at[pl.ds(0, TAIL), :], tx_s.at[0], tail_r.at[0], partner
    )
    tail_bc_in = remote(
        bcbuf.at[pl.ds(0, TAIL), :], bcbuf.at[pl.ds(0, TAIL), :], tb_s.at[0], tail_r.at[1], partner
    )
    tail_x_in.wait_recv()
    tail_bc_in.wait_recv()
    local[2].wait()
    local[3].wait()

    @pl.loop(1, PLANE)
    def _(r):
        dta_in(r).wait_recv()
        xa_in(r).wait_recv()

    sub = lax.broadcasted_iota(jnp.int32, (8, 1), 0)
    lane_head = lax.broadcasted_iota(jnp.int32, (1, WIDE), 1) // HEAD_P
    spread = (lax.broadcasted_iota(jnp.int32, (8, WIDE), 0) == lax.broadcasted_iota(jnp.int32, (8, WIDE), 1) // HEAD_P)
    spread = spread.astype(F32)
    a_log = jnp.zeros((8, 1), F32)
    skip = jnp.zeros((1, WIDE), F32)
    for h in range(OWN_HEADS):
        a_log = jnp.where(sub == h, alog_ref[j * OWN_HEADS + h], a_log)
        skip = jnp.where(lane_head == h, dskip_ref[j * OWN_HEADS + h], skip)
    rate = -jnp.exp(a_log)
    rows_i = lax.broadcasted_iota(jnp.int32, (ROWS, ROWS), 0)
    cols_i = lax.broadcasted_iota(jnp.int32, (ROWS, ROWS), 1)
    causal = cols_i <= rows_i
    sums = (rows_i <= cols_i).astype(F32)
    taps_x = taps_x_ref[:, cols(j)].astype(F32)
    taps_bc = taps_bc_ref[...].astype(F32)

    def conv(buf, taps, c):
        raw = buf[pl.ds(pl.multiple_of(c * ROWS, ROWS), ROWS + TAIL), :].astype(F32)
        row = lax.broadcasted_iota(jnp.int32, (ROWS + TAIL, 1), 0) + c * ROWS
        raw = jnp.where(jnp.logical_and(z == 0, row < TAIL), 0.0, raw)
        total = jnp.zeros((ROWS, WIDE), F32)
        for k in range(CONV):
            start = TAIL - CONV + 1 + k
            total = total + taps[k : k + 1, :] * raw[start : start + ROWS, :]
        return silu(total)

    def chunk(c):
        return pl.ds(pl.multiple_of(c * ROWS, ROWS), ROWS)

    def fore(c, carry):
        state, lead = carry
        xs = conv(xbuf, taps_x, c)
        xs_ref[chunk(c), :] = xs
        bc = conv(bcbuf, taps_bc, c)
        b_ref[chunk(c), :] = bc[:, :STATE]
        c_ref[chunk(c), :] = bc[:, STATE:]
        step = softplus(dtbuf[c])
        cum = exact(step * rate, sums)
        step_ref[c] = step
        cum_ref[c] = cum
        states[c] = state
        lead_ref[c] = jnp.broadcast_to(lead, (8, WIDE))
        end = cum[:, ROWS - 1 :]
        weight = exact(jnp.transpose(step * jnp.exp(end - cum)), spread)
        fade = exact(jnp.transpose(jnp.exp(jnp.broadcast_to(end, (8, ROWS)))), spread)[:1, :]
        state = state * fade + dot3(jnp.transpose(bc[:, :STATE]), xs * weight)
        return state, lead * fade

    state, lead = lax.fori_loop(
        0, PLANE, fore, (jnp.zeros((STATE, WIDE), F32), jnp.ones((1, WIDE), F32))
    )
    for k in range(PLANES):
        tsrc[k, pl.ds(0, SPLIT), :] = state[k * SPLIT : (k + 1) * SPLIT, :]
        tsrc[k, pl.ds(SPLIT, 8), :] = jnp.broadcast_to(lead, (8, WIDE))

    def ta(r):
        return remote(tsrc.at[(z + r) % PLANES], trecv.at[z], t_s.at[r], t_r.at[r], in_column(r))

    def ta_in(r):
        slot = trecv.at[from_column(r)]
        return remote(slot, slot, t_s.at[r], t_r.at[r], in_column(r))

    @pl.loop(1, PLANES)
    def _(r):
        ta(r).start()

    ring_step(1)

    def inside(c, _):
        xs = xs_ref[chunk(c), :]
        bmap = b_ref[chunk(c), :]
        cmap = c_ref[chunk(c), :]
        cum = cum_ref[c]
        step = step_ref[c]
        cum_t = jnp.transpose(cum)
        inner = dot3(cmap, bmap, NT)
        mixing = []
        blocks = []
        for h in range(OWN_HEADS):
            gap = cum_t[:, h : h + 1] - cum[h : h + 1, :]
            decay = jnp.where(causal, jnp.exp(jnp.where(causal, gap, 0.0)), 0.0)
            mixing.append(inner * decay * step[h : h + 1, :])
            blocks.append(jnp.where(lane_head == h, xs, 0.0))
        y = dot3(jnp.concatenate(mixing, axis=1), jnp.concatenate(blocks, axis=0))
        grown = exact(jnp.exp(cum_t), spread)
        y = y + grown * dot3(cmap, states[c]) + skip * xs
        y_ref[chunk(c), :] = y
        return 0

    trecv[z] = tsrc[z]
    lax.fori_loop(0, PLANE, inside, 0)

    @pl.loop(1, PLANES)
    def _(r):
        ta_in(r).wait_recv()

    def prefix(k, carry):
        psrc[k] = carry
        return carry * trecv[k, pl.ds(SPLIT, 1), :] + trecv[k, pl.ds(0, SPLIT), :]

    lax.fori_loop(0, PLANES, prefix, jnp.zeros((SPLIT, WIDE), F32))

    def part_rows(k):
        return pl.ds(pl.multiple_of(k * SPLIT, SPLIT), SPLIT)

    def pa(r):
        return remote(psrc.at[(z + r) % PLANES], precv.at[part_rows(z), :], p_s.at[r], p_r.at[r], in_column(r))

    def pa_in(r):
        slot = precv.at[part_rows(from_column(r)), :]
        return remote(slot, slot, p_s.at[r], p_r.at[r], in_column(r))

    @pl.loop(1, PLANES)
    def _(r):
        pa(r).start()

    precv[part_rows(z), :] = psrc[z]
    attend_step(1)
    ring_step(2)
    attend_step(7)

    @pl.loop(1, PLANES)
    def _(r):
        pa_in(r).wait_recv()

    local[4].wait()

    @pl.loop(1, PLANE)
    def _(r):
        ga_in(r).wait_recv()

    def finish(c, _):
        grown = exact(jnp.transpose(jnp.exp(cum_ref[c])), spread) * lead_ref[c][:1, :]
        y = y_ref[chunk(c), :] + grown * dot3(c_ref[chunk(c), :], precv[...])
        gated = y * silu(gbuf[chunk(c), :].astype(F32))
        y_ref[chunk(c), :] = gated
        ss_ref[pl.ds(c, 1), :] = exact(jnp.ones((8, WIDE), F32), gated * gated, NT)[:1, :]
        return 0

    lax.fori_loop(0, PLANE, finish, 0)

    def ma(r):
        return pltpu.make_async_remote_copy(
            src_ref=ss_ref,
            dst_ref=ssm_ref.at[r],
            send_sem=m_s.at[r],
            recv_sem=m_r.at[r],
            device_id={"mp": (mine_mp + r) % 4},
            device_id_type=MESH,
        )

    @pl.loop(1, 4)
    def _(r):
        ma(r).start()

    attend_step(2)
    ring_step(3)

    @pl.loop(1, 4)
    def _(r):
        ma(r).wait_recv()

    ss2_ref[...] = (ss_ref[...] + ssm_ref[1]) + (ssm_ref[2] + ssm_ref[3])

    def na(r):
        return remote(ss2_ref, ssp_ref.at[r], n_s.at[r], n_r.at[r], in_plane(r))

    @pl.loop(1, PLANE)
    def _(r):
        na(r).start()

    attend_step(6)

    @pl.loop(1, PLANE)
    def _(r):
        na(r).wait_recv()

    squares = ss2_ref[...]
    for r in range(1, PLANE):
        squares = squares + ssp_ref[r]
    inverse = jnp.transpose(lax.rsqrt(squares / D_INNER + 1e-05))
    gain = gain_ref[:, cols(j)]
    which = lax.broadcasted_iota(jnp.int32, (ROWS, PLANE), 1)

    def oa(r):
        return remote(osrc.at[r], mix_hbm.at[:, cols(j)], o_s.at[r], o_r.at[r], in_plane(r))

    def oa_in(r):
        return remote(osrc.at[r], mix_hbm.at[:, cols(from_plane(r))], o_s.at[r], o_r.at[r], in_plane(r))

    own_out = pltpu.make_async_copy(osrc.at[0], mix_hbm.at[:, cols(j)], local_sem.at[5])

    def norm(r, _):
        c = (j + r) % PLANE
        by = jnp.sum(jnp.where(which == c, inverse, 0.0), axis=1, keepdims=True)
        osrc[r] = (y_ref[chunk(c), :] * by * gain).astype(BF16)

        @pl.when(r > 0)
        def _():
            oa(r).start()

        return 0

    lax.fori_loop(0, PLANE, norm, 0)
    own_out.start()

    attend_step(3)
    ring_step(4)
    attend_step(5)
    attend_step(4)

    for h in range(Q_HEADS):
        acc = acc_ref[pl.ds(h * ROWS, ROWS), :]
        obuf[:, h * 128 : (h + 1) * 128] = (acc[:, :HEAD_WIDTH] / acc[:, HEAD_WIDTH:]).astype(BF16)
    att_out = pltpu.make_async_copy(obuf, att_hbm, local_sem.at[6])
    att_out.start()

    @pl.loop(1, CHIPS)
    def _(r):
        kvx(r).wait_send()
        bcx(r).wait_send()
        bcp(r).wait_send()
        ma(r).wait_send()

    bcp_own.wait_send()

    @pl.loop(1, PLANE)
    def _(r):
        dta(r).wait_send()
        xa(r).wait_send()
        ga(r).wait_send()
        ta(r).wait_send()
        pa(r).wait_send()
        na(r).wait_send()
        oa(r).wait_send()

    @pl.when(j == PLANE - 1)
    def _():
        @pl.loop(0, PLANE)
        def _(d):
            tail_x(d).wait_send()
            tail_bc(d).wait_send()

    for s in range(1, 5):
        up(s).wait_send()
    for s in range(1, 4):
        down(s).wait_send()
    for i in range(PLANES):
        share((z + PLANES - i) % PLANES, i).wait_send()

    @pl.loop(1, PLANE)
    def _(r):
        oa_in(r).wait_recv()

    own_out.wait()
    att_out.wait()


def body(
    x_in, gate_z, bc_in, dt_raw, a_log, d_skip, conv_x, conv_bc, norm_gain, queries, key_value_pairs
):
    anywhere = pl.BlockSpec(memory_space=pl.ANY)
    vmem = pl.BlockSpec(memory_space=pltpu.VMEM)
    smem = pl.BlockSpec(memory_space=pltpu.SMEM)
    dma = pltpu.SemaphoreType.DMA
    scratch = [
        pltpu.VMEM((PLANES, 2, TOK, HEAD_WIDTH), BF16),
        pltpu.VMEM((TAIL + TOK, WIDE), BF16),
        pltpu.VMEM((TOK, WIDE), BF16),
        pltpu.VMEM((TAIL + TOK, WIDE), BF16),
        pltpu.VMEM((PLANE, 8, ROWS), F32),
        pltpu.VMEM((PLANE, 8, ROWS), F32),
        pltpu.VMEM((TOK, WIDE), F32),
        pltpu.VMEM((TOK, STATE), F32),
        pltpu.VMEM((TOK, STATE), F32),
        pltpu.VMEM((PLANE, 8, ROWS), F32),
        pltpu.VMEM((PLANE, 8, ROWS), F32),
        pltpu.VMEM((PLANE, 8, WIDE), F32),
        pltpu.VMEM((PLANE, STATE, WIDE), F32),
        pltpu.VMEM((TOK, WIDE), F32),
        pltpu.VMEM((PLANES, SPLIT + 8, WIDE), F32),
        pltpu.VMEM((PLANES, SPLIT + 8, WIDE), F32),
        pltpu.VMEM((PLANES, SPLIT, WIDE), F32),
        pltpu.VMEM((STATE, WIDE), F32),
        pltpu.VMEM((PLANE, ROWS), F32),
        pltpu.VMEM((4, PLANE, ROWS), F32),
        pltpu.VMEM((PLANE, ROWS), F32),
        pltpu.VMEM((PLANE, PLANE, ROWS), F32),
        pltpu.VMEM((PLANE, ROWS, WIDE), BF16),
        pltpu.VMEM((Q_HEADS * ROWS, HEAD_WIDTH), BF16),
        pltpu.VMEM((Q_HEADS * ROWS, HEAD_WIDTH), F32),
        pltpu.VMEM((Q_HEADS * ROWS, 2 * HEAD_WIDTH), F32),
        pltpu.VMEM((ROWS, Q_HEADS * HEAD_WIDTH), BF16),
        dma((7,)),
        dma((Q_HEADS,)),
        dma((8,)),
        dma((8,)),
        dma((8,)),
        dma((8,)),
        dma((8,)),
        dma((8,)),
        dma((4,)),
        dma((4,)),
        dma((4,)),
        dma((4,)),
        dma((4,)),
        dma((4,)),
        dma((8,)),
        dma((8,)),
        dma((5,)),
        dma((5,)),
        dma((4,)),
        dma((4,)),
        dma((8,)),
        dma((8,)),
        dma((2,)),
        dma((8,)),
        dma((8,)),
        dma((8,)),
        dma((8,)),
        dma((4,)),
        dma((4,)),
        dma((8,)),
        dma((8,)),
        dma((8,)),
        dma((8,)),
    ]
    return pl.pallas_call(
        kernel,
        out_shape=(
            jax.ShapeDtypeStruct(x_in.shape, BF16),
            jax.ShapeDtypeStruct(queries.shape, BF16),
        ),
        in_specs=[
            anywhere,
            anywhere,
            anywhere,
            vmem,
            smem,
            smem,
            vmem,
            vmem,
            vmem,
            anywhere,
            anywhere,
        ],
        out_specs=(anywhere, anywhere),
        scratch_shapes=scratch,
        compiler_params=pltpu.CompilerParams(
            collective_id=0, has_side_effects=True, vmem_limit_bytes=60 * 1024 * 1024
        ),
    )(
        x_in,
        gate_z,
        bc_in,
        dt_raw,
        a_log,
        d_skip,
        conv_x,
        conv_bc,
        norm_gain[None, :],
        queries,
        key_value_pairs,
    )


def solution(mesh):
    placed = (
        P("seq", "mp"),
        P("seq", "mp"),
        P("seq", None),
        P("seq", "mp"),
        P("mp"),
        P("mp"),
        P(None, "mp"),
        P(),
        P("mp"),
        P("seq", "mp"),
        P(None, "seq", "mp"),
    )
    return jax.shard_map(
        body,
        mesh=mesh,
        in_specs=placed,
        out_specs=(P("seq", "mp"), P("seq", "mp")),
        check_vma=False,
    )
```

time: 436 us -> 84.6 us (0.19); the launches traced: 427 us -> 84.3 us
  waiting for transfers between devices: 162 us -> 0 us
  matrix products: 144 us -> 0 us
  Pallas kernels: 0 us -> 79.6 us
  blocking collectives: 44.7 us -> 0 us
  local copies, waits for them, and re-layouts: 28.3 us -> 4.08 us
  other arithmetic: 17.3 us -> 0 us
  between operations: 14.3 us -> 0.65 us
  loops' own time: 10.9 us -> 0 us
  starting transfers between devices: 5.66 us -> 0 us
    all_gather x2 -> x0, waiting for transfers between devices: 162 us -> none  [the longest x1 136 us: body(): lax.all_gather(s_loc[None], 'seq', axis=0, tiled=True)]
    dot_general x21 -> x0, matrix products: 143 us -> none  [the longest x1 82.2 us: body(): jnp.einsum('kh,khnp->hnp', weights, lax.all_gather(s_loc[None], 'seq', ax...]
    pallas_call x0 -> x1, Pallas kernels: none -> 79.6 us  [body(): pl.pallas_call(kernel, out_shape=(jax.ShapeDtypeStruct(x_in.shape, BF16),...]
    all_gather x1 -> x0, blocking collectives: 38.1 us -> none  [body(): logs = lax.all_gather(cum[-1][None, :], 'seq', axis=0, tiled=True)]
    cond x24 -> x0, local copies, waits for them, and re-layouts: 15.5 us -> none
    another operation x9 -> x0, loops' own time: 10.9 us -> none  [the longest x1 10.3 us: attend(): lax.scan(visit, start_state, (jnp.arange(length // span, dtype=jnp.int32)...]
    reduce_sum x9 -> x0, other arithmetic: 7.33 us -> none  [the longest x8 6.9 us: update(): total = total * fade + jnp.sum(weights, axis=-1)]
    psum x1 -> x0, blocking collectives: 6.59 us -> none  [body(): squares = lax.psum(jnp.sum(gated * gated, axis=1), 'mp')]
  transfers between devices with their start and end apart: 4 -> 0, of which waited for: 2 -> 0; matrix products, arithmetic and copies ran while one was open for 20% -> 0% of each run, Pallas kernels for 0% -> 0%
where the time goes in v1:
time: 84.6 us; the launch traced here: 84.3 us
  Pallas kernels  79.6 us (94%)
  local copies, waits for them, and re-layouts  4.08 us (5%)
    pallas_call x1, Pallas kernels, body(): pl.pallas_call(kernel, out_shape=(jax.ShapeDtypeStruct(x_in.shape, BF16),...  79.6 us
    unnamed x5, local copies, waits for them, and re-layouts  4.08 us

profile of v1, /device:TPU:233, one launch (start us, length us, event | category | flops | bytes accessed | tf_op | source)
XLA Modules:
  0.0 84.3 jit_solution(8000143486228172266)
XLA Ops:
  0.6 1.4 %copy.13.dt_ref = f32[128,32]{1,0:T(8,128)} copy(f32[128,32]{0,1:T(8,128)} %param.14) | data formatting | bytes 32768 | tf_op args[3]
  2.1 79.6 %shard_map.122 = (bf16[128,2048]{1,0:T(8,128)(2,1)}, bf16[128,1024]{1,0:T(8,128)(2,1)}) custom-call(bf16[128,2048]{1,0:T(8,128)(2,1)} %x_hbm.1, bf16[128,2048]{1,0:T(8,128)(2,1)} %gate_hbm.1, bf16[128,256]{1,0:T(8,128)(2,1)} %bc_hbm.1, f32[128,32]{1,0:T(8,128)} %copy.13.dt_ref, f32[32]{0:T(128)} %alog_ref.1, f32[32]{0:T(128)} %dskip_ref.1, ...), custom_call_target="tpu_custom_call" | custom-call | tf_op jit(solution)/shard_map/pallas_call | solution.py:758
  81.7 0.0 copy-start
  81.7 1.9 %copy.16 = bf16[128,2048]{1,0:T(8,128)(2,1)} copy(bf16[128,2048]{1,0:T(8,128)(2,1)} %get-tuple-element.4) | data formatting | bytes 1048576
  83.6 0.0 copy-done
  83.6 0.7 copy.17
Async XLA Ops:
  81.7 1.9 %copy-start = (bf16[128,1024]{1,0:T(8,128)(2,1)S(1)}, bf16[128,1024]{1,0:T(8,128)(2,1)}, u32[]{:S(2)}) copy-start(bf16[128,1024]{1,0:T(8,128)(2,1)} %get-tuple-element.5) | copy-start | bytes 786436

commit v2 on v1

--- a/solution.py
+++ b/solution.py
@@ -25,17 +25,12 @@
 MESH = pl.DeviceIdType.MESH
 F32 = jnp.float32
 BF16 = jnp.bfloat16
-HI = lax.Precision.HIGHEST
 NN = (((1,), (0,)), ((), ()))
 NT = (((1,), (1,)), ((), ()))
 
 
 def dot1(a, b, dims=NN):
     return lax.dot_general(a, b, dims, preferred_element_type=F32)
-
-
-def exact(a, b, dims=NN):
-    return lax.dot_general(a, b, dims, precision=HI, preferred_element_type=F32)
 
 
 def halves(v):
@@ -43,10 +38,33 @@
     return high, (v - high.astype(F32)).astype(BF16)
 
 
+def left3(a):
+    high, low = halves(a)
+    return jnp.concatenate([high, low, high], axis=1)
+
+
+def right3(b, axis):
+    high, low = halves(b)
+    return jnp.concatenate([high, high, low], axis=axis)
+
+
 def dot3(a, b, dims=NN):
-    ah, al = halves(a)
-    bh, bl = halves(b)
-    return dot1(ah, bh, dims) + (dot1(ah, bl, dims) + dot1(al, bh, dims))
+    return dot1(left3(a), right3(b, 0 if dims == NN else 1), dims)
+
+
+def widen(rows, spread):
+    high = rows.astype(BF16).astype(F32)
+    both = jnp.concatenate([high, rows - high], axis=0)
+    return dot1(jnp.transpose(both).astype(BF16), spread)
+
+
+def running_sums(rows, sums):
+    high = rows.astype(BF16).astype(F32)
+    rest = rows - high
+    middle = rest.astype(BF16).astype(F32)
+    parts = jnp.concatenate([high, middle, rest - middle], axis=0).astype(BF16)
+    total = dot1(parts, sums)
+    return total[:8] + (total[8:16] + total[16:])
 
 
 def silu(v):
@@ -87,6 +105,7 @@
     cum_ref,
     step_ref,
     lead_ref,
+    grown_ref,
     states,
     y_ref,
     tsrc,
@@ -94,8 +113,6 @@
     psrc,
     precv,
     ss_ref,
-    ssm_ref,
-    ss2_ref,
     ssp_ref,
     osrc,
     qbuf,
@@ -129,8 +146,6 @@
     t_r,
     p_s,
     p_r,
-    m_s,
-    m_r,
     n_s,
     n_r,
     o_s,
@@ -172,14 +187,18 @@
     def greet(seq):
         pl.semaphore_signal(barrier, inc=1, device_id={"seq": seq}, device_id_type=MESH)
 
+    @pl.loop(1, 4 * PLANE)
+    def _(q):
+        pl.semaphore_signal(
+            barrier,
+            inc=1,
+            device_id={"seq": in_plane(q % PLANE), "mp": (mine_mp + q // PLANE) % 4},
+            device_id_type=MESH,
+        )
+
     @pl.loop(1, PLANE)
     def _(r):
-        greet(in_plane(r))
         greet(in_column(r))
-
-    @pl.loop(1, 4)
-    def _(r):
-        pl.semaphore_signal(barrier, inc=1, device_id={"mp": (mine_mp + r) % 4}, device_id_type=MESH)
 
     @pl.when(j == PLANE - 1)
     def _():
@@ -191,7 +210,7 @@
     def _():
         greet(below + PLANE - 1)
 
-    dt_t = jnp.transpose(dt_ref[...])
+    dt_t = dt_ref[...]
     for d in range(PLANE):
         dtsrc[d, pl.ds(0, OWN_HEADS), :] = dt_t[d * OWN_HEADS : (d + 1) * OWN_HEADS]
         dtsrc[d, pl.ds(OWN_HEADS, OWN_HEADS), :] = jnp.zeros((OWN_HEADS, ROWS), F32)
@@ -217,7 +236,7 @@
     for h in range(Q_HEADS):
         pltpu.make_async_copy(q_hbm.at[:, pl.ds(h * 128, 128)], qbuf.at[pl.ds(h * ROWS, ROWS), :], q_sem.at[h]).start()
 
-    pl.semaphore_wait(barrier, 2 * (PLANE - 1) + 3 + jnp.where(j == PLANE - 1, PLANE - 1, 1))
+    pl.semaphore_wait(barrier, 5 * PLANE - 2 + jnp.where(j == PLANE - 1, PLANE - 1, 1))
 
     def kvx(r):
         return remote(kv_hbm, kv_mine, kvx_s.at[r], kvx_r.at[r], on_chip(r))
@@ -359,7 +378,7 @@
             share((z + s) % PLANES, 8 - s).start()
 
     factor = (HEAD_WIDTH ** (-0.5)) * 1.4426950408889634
-    tile = 256
+    tile = 512
 
     def attend(zz, own):
         @pl.loop(0, Q_HEADS * ROWS // tile)
@@ -429,8 +448,8 @@
 
     sub = lax.broadcasted_iota(jnp.int32, (8, 1), 0)
     lane_head = lax.broadcasted_iota(jnp.int32, (1, WIDE), 1) // HEAD_P
-    spread = (lax.broadcasted_iota(jnp.int32, (8, WIDE), 0) == lax.broadcasted_iota(jnp.int32, (8, WIDE), 1) // HEAD_P)
-    spread = spread.astype(F32)
+    spread = lax.broadcasted_iota(jnp.int32, (16, WIDE), 0) % 8 == lax.broadcasted_iota(jnp.int32, (16, WIDE), 1) // HEAD_P
+    spread = spread.astype(F32).astype(BF16)
     a_log = jnp.zeros((8, 1), F32)
     skip = jnp.zeros((1, WIDE), F32)
     for h in range(OWN_HEADS):
@@ -440,7 +459,7 @@
     rows_i = lax.broadcasted_iota(jnp.int32, (ROWS, ROWS), 0)
     cols_i = lax.broadcasted_iota(jnp.int32, (ROWS, ROWS), 1)
     causal = cols_i <= rows_i
-    sums = (rows_i <= cols_i).astype(F32)
+    sums = (rows_i <= cols_i).astype(F32).astype(BF16)
     taps_x = taps_x_ref[:, cols(j)].astype(F32)
     taps_bc = taps_bc_ref[...].astype(F32)
 
@@ -465,14 +484,16 @@
         b_ref[chunk(c), :] = bc[:, :STATE]
         c_ref[chunk(c), :] = bc[:, STATE:]
         step = softplus(dtbuf[c])
-        cum = exact(step * rate, sums)
+        cum = running_sums(step * rate, sums)
         step_ref[c] = step
         cum_ref[c] = cum
         states[c] = state
         lead_ref[c] = jnp.broadcast_to(lead, (8, WIDE))
         end = cum[:, ROWS - 1 :]
-        weight = exact(jnp.transpose(step * jnp.exp(end - cum)), spread)
-        fade = exact(jnp.transpose(jnp.exp(jnp.broadcast_to(end, (8, ROWS)))), spread)[:1, :]
+        weight = widen(step * jnp.exp(end - cum), spread)
+        grown = widen(jnp.exp(cum), spread)
+        grown_ref[chunk(c), :] = grown
+        fade = grown[ROWS - 1 :, :]
         state = state * fade + dot3(jnp.transpose(bc[:, :STATE]), xs * weight)
         return state, lead * fade
 
@@ -512,8 +533,7 @@
             mixing.append(inner * decay * step[h : h + 1, :])
             blocks.append(jnp.where(lane_head == h, xs, 0.0))
         y = dot3(jnp.concatenate(mixing, axis=1), jnp.concatenate(blocks, axis=0))
-        grown = exact(jnp.exp(cum_t), spread)
-        y = y + grown * dot3(cmap, states[c]) + skip * xs
+        y = y + grown_ref[chunk(c), :] * dot3(cmap, states[c]) + skip * xs
         y_ref[chunk(c), :] = y
         return 0
 
@@ -559,58 +579,45 @@
     def _(r):
         ga_in(r).wait_recv()
 
-    def finish(c, _):
-        grown = exact(jnp.transpose(jnp.exp(cum_ref[c])), spread) * lead_ref[c][:1, :]
-        y = y_ref[chunk(c), :] + grown * dot3(c_ref[chunk(c), :], precv[...])
+    which = lax.broadcasted_iota(jnp.int32, (ROWS, PLANE), 1)
+    before = right3(precv[...], 0)
+
+    def finish(c, squares):
+        grown = grown_ref[chunk(c), :] * lead_ref[c][:1, :]
+        y = y_ref[chunk(c), :] + grown * dot1(left3(c_ref[chunk(c), :]), before)
         gated = y * silu(gbuf[chunk(c), :].astype(F32))
         y_ref[chunk(c), :] = gated
-        ss_ref[pl.ds(c, 1), :] = exact(jnp.ones((8, WIDE), F32), gated * gated, NT)[:1, :]
-        return 0
-
-    lax.fori_loop(0, PLANE, finish, 0)
-
-    def ma(r):
+        return jnp.where(which == c, jnp.sum(gated * gated, axis=1, keepdims=True), squares)
+
+    ss_ref[...] = jnp.transpose(lax.fori_loop(0, PLANE, finish, jnp.zeros((ROWS, PLANE), F32)))
+
+    def na(q):
         return pltpu.make_async_remote_copy(
             src_ref=ss_ref,
-            dst_ref=ssm_ref.at[r],
-            send_sem=m_s.at[r],
-            recv_sem=m_r.at[r],
-            device_id={"mp": (mine_mp + r) % 4},
+            dst_ref=ssp_ref.at[q],
+            send_sem=n_s.at[q],
+            recv_sem=n_r.at[q],
+            device_id={"seq": in_plane(q % PLANE), "mp": (mine_mp + q // PLANE) % 4},
             device_id_type=MESH,
         )
 
-    @pl.loop(1, 4)
-    def _(r):
-        ma(r).start()
+    @pl.loop(1, 4 * PLANE)
+    def _(q):
+        na(q).start()
 
     attend_step(2)
     ring_step(3)
-
-    @pl.loop(1, 4)
-    def _(r):
-        ma(r).wait_recv()
-
-    ss2_ref[...] = (ss_ref[...] + ssm_ref[1]) + (ssm_ref[2] + ssm_ref[3])
-
-    def na(r):
-        return remote(ss2_ref, ssp_ref.at[r], n_s.at[r], n_r.at[r], in_plane(r))
-
-    @pl.loop(1, PLANE)
-    def _(r):
-        na(r).start()
-
     attend_step(6)
 
-    @pl.loop(1, PLANE)
-    def _(r):
-        na(r).wait_recv()
-
-    squares = ss2_ref[...]
-    for r in range(1, PLANE):
-        squares = squares + ssp_ref[r]
+    @pl.loop(1, 4 * PLANE)
+    def _(q):
+        na(q).wait_recv()
+
+    squares = ss_ref[...]
+    for q in range(1, 4 * PLANE):
+        squares = squares + ssp_ref[q]
     inverse = jnp.transpose(lax.rsqrt(squares / D_INNER + 1e-05))
     gain = gain_ref[:, cols(j)]
-    which = lax.broadcasted_iota(jnp.int32, (ROWS, PLANE), 1)
 
     def oa(r):
         return remote(osrc.at[r], mix_hbm.at[:, cols(j)], o_s.at[r], o_r.at[r], in_plane(r))
@@ -650,9 +657,12 @@
         kvx(r).wait_send()
         bcx(r).wait_send()
         bcp(r).wait_send()
-        ma(r).wait_send()
 
     bcp_own.wait_send()
+
+    @pl.loop(1, 4 * PLANE)
+    def _(q):
+        na(q).wait_send()
 
     @pl.loop(1, PLANE)
     def _(r):
@@ -661,7 +671,6 @@
         ga(r).wait_send()
         ta(r).wait_send()
         pa(r).wait_send()
-        na(r).wait_send()
         oa(r).wait_send()
 
     @pl.when(j == PLANE - 1)
@@ -706,6 +715,7 @@
         pltpu.VMEM((PLANE, 8, ROWS), F32),
         pltpu.VMEM((PLANE, 8, ROWS), F32),
         pltpu.VMEM((PLANE, 8, WIDE), F32),
+        pltpu.VMEM((TOK, WIDE), F32),
         pltpu.VMEM((PLANE, STATE, WIDE), F32),
         pltpu.VMEM((TOK, WIDE), F32),
         pltpu.VMEM((PLANES, SPLIT + 8, WIDE), F32),
@@ -713,9 +723,7 @@
         pltpu.VMEM((PLANES, SPLIT, WIDE), F32),
         pltpu.VMEM((STATE, WIDE), F32),
         pltpu.VMEM((PLANE, ROWS), F32),
-        pltpu.VMEM((4, PLANE, ROWS), F32),
-        pltpu.VMEM((PLANE, ROWS), F32),
-        pltpu.VMEM((PLANE, PLANE, ROWS), F32),
+        pltpu.VMEM((4 * PLANE, PLANE, ROWS), F32),
         pltpu.VMEM((PLANE, ROWS, WIDE), BF16),
         pltpu.VMEM((Q_HEADS * ROWS, HEAD_WIDTH), BF16),
         pltpu.VMEM((Q_HEADS * ROWS, HEAD_WIDTH), F32),
@@ -748,10 +756,8 @@
         dma((8,)),
         dma((8,)),
         dma((8,)),
-        dma((4,)),
-        dma((4,)),
-        dma((8,)),
-        dma((8,)),
+        dma((32,)),
+        dma((32,)),
         dma((8,)),
         dma((8,)),
     ]
@@ -783,7 +789,7 @@
         x_in,
         gate_z,
         bc_in,
-        dt_raw,
+        dt_raw.T,
         a_log,
         d_skip,
         conv_x,

time: 84.6 us -> 76.8 us (0.908)
  Pallas kernels: 79.6 us -> 73.4 us
  local copies, waits for them, and re-layouts: 4.08 us -> 2.63 us
    pallas_call x1, Pallas kernels: 79.6 us -> 73.4 us  [body(): pl.pallas_call(kernel, out_shape=(jax.ShapeDtypeStruct(x_in.shape, BF16),...]
    unnamed x5 -> x4, local copies, waits for them, and re-layouts: 4.08 us -> 2.63 us
where the time goes in v2:
time: 76.8 us; the launch traced here: 76.7 us
  Pallas kernels  73.4 us (96%)
  local copies, waits for them, and re-layouts  2.63 us (3%)
    pallas_call x1, Pallas kernels, body(): pl.pallas_call(kernel, out_shape=(jax.ShapeDtypeStruct(x_in.shape, BF16),...  73.4 us
    unnamed x4, local copies, waits for them, and re-layouts  2.63 us

profile of v2, /device:TPU:233, one launch (start us, length us, event | category | flops | bytes accessed | tf_op | source)
XLA Modules:
  0.0 76.7 jit_solution(713320319232725544)
XLA Ops:
  0.6 73.4 %shard_map.122 = (bf16[128,2048]{1,0:T(8,128)(2,1)}, bf16[128,1024]{1,0:T(8,128)(2,1)}) custom-call(bf16[128,2048]{1,0:T(8,128)(2,1)} %x_hbm.1, bf16[128,2048]{1,0:T(8,128)(2,1)} %gate_hbm.1, bf16[128,256]{1,0:T(8,128)(2,1)} %bc_hbm.1, f32[32,128]{1,0:T(8,128)} %bitcast.2, f32[32]{0:T(128)} %alog_ref.1, f32[32]{0:T(128)} %dskip_ref.1, ...), custom_call_target="tpu_custom_call" | custom-call | tf_op jit(solution)/shard_map/pallas_call | solution.py:764
  74.0 0.0 copy-start
  74.0 1.9 %copy.15 = bf16[128,2048]{1,0:T(8,128)(2,1)} copy(bf16[128,2048]{1,0:T(8,128)(2,1)} %get-tuple-element.4) | data formatting | bytes 1048576
  75.9 0.0 copy-done
  76.0 0.7 copy.16
Async XLA Ops:
  74.0 1.9 %copy-start = (bf16[128,1024]{1,0:T(8,128)(2,1)S(1)}, bf16[128,1024]{1,0:T(8,128)(2,1)}, u32[]{:S(2)}) copy-start(bf16[128,1024]{1,0:T(8,128)(2,1)} %get-tuple-element.5) | copy-start | bytes 786436
